TPU v7x, 32 devices: a whole 2x2x4 slice. The times are simulated.
32 devices in a mesh: fsdp: 16 (over z, y, core), seq: 2 (over x).
Axes of the slice: x: 2, y: 2, z: 4, core: 2. Of those that a mesh axis runs over, the one named last changes fastest.
Arguments:
- block_input: bfloat16 [2, 16, 1024, 1024], P(None, 'fsdp', 'seq'), may hold values from -6 to 6
- output_grad: bfloat16 [2, 16, 1024, 1024], P(None, 'fsdp', 'seq'), may hold values from -6 to 6
- adapter_ids: int32 [2, 16], P(None, 'fsdp'), may hold values from 0 to 7
- in_weight: bfloat16 [1024, 3072], P('fsdp'), may hold values from -0.1875 to 0.1875
- out_weight: bfloat16 [1024, 1024], P('fsdp'), may hold values from -0.1875 to 0.1875
- gate_weight: bfloat16 [1024, 4608], P('fsdp'), may hold values from -0.1875 to 0.1875
- up_weight: bfloat16 [1024, 4608], P('fsdp'), may hold values from -0.1875 to 0.1875
- down_weight: bfloat16 [4608, 1024], P('fsdp'), may hold values from -0.09375 to 0.09375
- conv_weight: bfloat16 [3, 1024], replicated, may hold values from -3.5 to 3.5
- first_gain: bfloat16 [1024], replicated, may hold values from 0.099609375 to 1.8984375
- second_gain: bfloat16 [1024], replicated, may hold values from 0.099609375 to 1.8984375
- infirst_adapter: bfloat16 [1024, 128], replicated, may hold values from -0.1875 to 0.1875
- insecond_adapter: bfloat16 [128, 3072], replicated, may hold values from -1.5 to 1.5
- outfirst_adapter: bfloat16 [1024, 128], replicated, may hold values from -0.1875 to 0.1875
- outsecond_adapter: bfloat16 [128, 1024], replicated, may hold values from -1.5 to 1.5
- gatefirst_adapter: bfloat16 [1024, 128], replicated, may hold values from -0.1875 to 0.1875
- gatesecond_adapter: bfloat16 [128, 4608], replicated, may hold values from -1.5 to 1.5
- upfirst_adapter: bfloat16 [1024, 128], replicated, may hold values from -0.1875 to 0.1875
- upsecond_adapter: bfloat16 [128, 4608], replicated, may hold values from -1.5 to 1.5
- downfirst_adapter: bfloat16 [4608, 128], replicated, may hold values from -0.09375 to 0.09375
- downsecond_adapter: bfloat16 [128, 1024], replicated, may hold values from -1.5 to 1.5
Outputs:
- block_output: bfloat16 [2, 16, 1024, 1024], P(None, 'fsdp', 'seq')
- input_grad: bfloat16 [2, 16, 1024, 1024], P(None, 'fsdp', 'seq')
- infirst_grad: float32 [1024, 128], replicated
- insecond_grad: float32 [128, 3072], replicated
- outfirst_grad: float32 [1024, 128], replicated
- outsecond_grad: float32 [128, 1024], replicated
- gatefirst_grad: float32 [1024, 128], replicated
- gatesecond_grad: float32 [128, 4608], replicated
- upfirst_grad: float32 [1024, 128], replicated
- upsecond_grad: float32 [128, 4608], replicated
- downfirst_grad: float32 [4608, 128], replicated
- downsecond_grad: float32 [128, 1024], replicated
All inputs are finite; a program needn't handle non-finite values.
Results may differ from a plain program's by a relative error of at most 0.012.
The roundings to bfloat16 on the way count: a program that leaves them out, or rounds other values in their place, can miss the bound.
Values may be sent and summed in bfloat16 or wider, within the bound.
A program may use at most 256 MiB of HBM per device.

v0:
```python
import jax
import jax.numpy as jnp
from jax import lax
from jax.sharding import PartitionSpec as P

R = 16
EPSILON = 1e-05
ADAPTER_SCALE = 0.5


def from_behind(block, axis, distance):
    devices = range(lax.axis_size(axis))
    route = [(i - distance, i) for i in devices if i - distance in devices]
    return lax.ppermute(block, axis, route)


def forward_dot(left_side, right_side):
    return jnp.dot(left_side, right_side, preferred_element_type=jnp.float32)


def against_dot(left_side, right_side):
    return lax.dot_general(
        left_side, right_side, (((1,), (1,)), ((), ())), preferred_element_type=jnp.float32
    )


def outer_dot(left_side, right_side):
    return lax.dot_general(
        left_side, right_side, (((0,), (0,)), ((), ())), preferred_element_type=jnp.float32
    )


def adapted(inputs, weight, first_map, second_map, select):
    reduced = forward_dot(inputs, first_map).astype(jnp.bfloat16) * select
    result = forward_dot(inputs, weight) + ADAPTER_SCALE * forward_dot(reduced, second_map)
    return (result, reduced)


def adapted_back(grad_low, inputs, reduced, weight, first_map, second_map, select):
    grad_second = ADAPTER_SCALE * outer_dot(reduced, grad_low)
    grad_reduced = (ADAPTER_SCALE * against_dot(grad_low, second_map) * select).astype(jnp.bfloat16)
    grad_first = outer_dot(inputs, grad_reduced)
    grad_inputs = against_dot(grad_low, weight) + against_dot(grad_reduced, first_map)
    return (grad_inputs, grad_first, grad_second)


def rms_parts(values):
    inverse = lax.rsqrt(jnp.mean(values * values, axis=-1, keepdims=True) + EPSILON)
    return (inverse, values * inverse)


def rms_back(grad_normed, gain_vector, inverse, unit_rows):
    scaled = grad_normed * gain_vector
    return inverse * (scaled - unit_rows * jnp.mean(scaled * unit_rows, axis=-1, keepdims=True))


def per_device(
    block_input,
    output_grad,
    adapter_ids,
    in_weight,
    out_weight,
    gate_weight,
    up_weight,
    down_weight,
    conv_weight,
    first_gain,
    second_gain,
    infirst_adapter,
    insecond_adapter,
    outfirst_adapter,
    outsecond_adapter,
    gatefirst_adapter,
    gatesecond_adapter,
    upfirst_adapter,
    upsecond_adapter,
    downfirst_adapter,
    downsecond_adapter,
):
    batches, seq_count, local_len, features = block_input.shape
    row_count = seq_count * local_len
    adapters = (
        infirst_adapter,
        insecond_adapter,
        outfirst_adapter,
        outsecond_adapter,
        gatefirst_adapter,
        gatesecond_adapter,
        upfirst_adapter,
        upsecond_adapter,
        downfirst_adapter,
        downsecond_adapter,
    )
    slot_count = infirst_adapter.shape[1]
    kernel = conv_weight.astype(jnp.float32)
    gain_first = first_gain.astype(jnp.float32)
    gain_second = second_gain.astype(jnp.float32)
    owners = lax.broadcasted_iota(jnp.int32, (1, 1, slot_count), 2) // R
    totals = [jnp.zeros(member.shape, jnp.float32) for member in adapters]
    outputs = []
    input_grads = []
    for batch_index in range(batches):
        weight_in, weight_out, weight_gate, weight_up, weight_down = (
            lax.all_gather(in_weight, "fsdp", axis=0, tiled=True),
            lax.all_gather(out_weight, "fsdp", axis=0, tiled=True),
            lax.all_gather(gate_weight, "fsdp", axis=0, tiled=True),
            lax.all_gather(up_weight, "fsdp", axis=0, tiled=True),
            lax.all_gather(down_weight, "fsdp", axis=0, tiled=True),
        )
        inputs = block_input[batch_index].reshape(row_count, features).astype(jnp.float32)
        matches = owners == adapter_ids[batch_index][:, None, None]
        select = (
            jnp.broadcast_to(matches, (seq_count, local_len, slot_count))
            .reshape(row_count, slot_count)
            .astype(jnp.bfloat16)
        )
        inverse_first, unit_first = rms_parts(inputs)
        normed = (unit_first * gain_first).astype(jnp.bfloat16)
        mixed_in, low_in = adapted(normed, weight_in, adapters[0], adapters[1], select)
        first_part = mixed_in[:, :features]
        middle_part = mixed_in[:, features : 2 * features]
        last_part = mixed_in[:, 2 * features :]
        gated_values = (first_part * last_part).reshape(seq_count, local_len, features)
        rim_rows = from_behind(gated_values[:, local_len - 2 :, :], "seq", 1)
        extended = jnp.concatenate([rim_rows, gated_values], axis=1)
        conv_out = (
            kernel[0] * extended[:, :local_len]
            + kernel[1] * extended[:, 1 : local_len + 1]
            + kernel[2] * extended[:, 2:]
        ).reshape(row_count, features)
        mixer_out = (middle_part * conv_out).astype(jnp.bfloat16)
        branch, low_out = adapted(mixer_out, weight_out, adapters[2], adapters[3], select)
        after_mixer = inputs + branch
        inverse_second, unit_second = rms_parts(after_mixer)
        second = (unit_second * gain_second).astype(jnp.bfloat16)
        gate_value, low_gate = adapted(second, weight_gate, adapters[4], adapters[5], select)
        up_value, low_up = adapted(second, weight_up, adapters[6], adapters[7], select)
        sigmoid_gate = jax.nn.sigmoid(gate_value)
        activated = gate_value * sigmoid_gate
        hidden = (activated * up_value).astype(jnp.bfloat16)
        down_value, low_down = adapted(hidden, weight_down, adapters[8], adapters[9], select)
        outputs.append(
            (after_mixer + down_value).astype(jnp.bfloat16).reshape(seq_count, local_len, features)
        )
        weight_in, weight_out, weight_gate, weight_up, weight_down = (
            lax.all_gather(in_weight, "fsdp", axis=0, tiled=True),
            lax.all_gather(out_weight, "fsdp", axis=0, tiled=True),
            lax.all_gather(gate_weight, "fsdp", axis=0, tiled=True),
            lax.all_gather(up_weight, "fsdp", axis=0, tiled=True),
            lax.all_gather(down_weight, "fsdp", axis=0, tiled=True),
        )
        cotangent = output_grad[batch_index].reshape(row_count, features)
        grad_hidden, grad_first, grad_second = adapted_back(
            cotangent, hidden, low_down, weight_down, adapters[8], adapters[9], select
        )
        totals[8] = totals[8] + grad_first
        totals[9] = totals[9] + grad_second
        grad_gate = (
            grad_hidden * up_value * sigmoid_gate * (1.0 + gate_value * (1.0 - sigmoid_gate))
        ).astype(jnp.bfloat16)
        grad_upper = (grad_hidden * activated).astype(jnp.bfloat16)
        back_gate, grad_first, grad_second = adapted_back(
            grad_gate, second, low_gate, weight_gate, adapters[4], adapters[5], select
        )
        totals[4] = totals[4] + grad_first
        totals[5] = totals[5] + grad_second
        back_upper, grad_first, grad_second = adapted_back(
            grad_upper, second, low_up, weight_up, adapters[6], adapters[7], select
        )
        totals[6] = totals[6] + grad_first
        totals[7] = totals[7] + grad_second
        grad_after = cotangent.astype(jnp.float32) + rms_back(
            back_gate + back_upper, gain_second, inverse_second, unit_second
        )
        grad_mixer, grad_first, grad_second = adapted_back(
            grad_after.astype(jnp.bfloat16),
            mixer_out,
            low_out,
            weight_out,
            adapters[2],
            adapters[3],
            select,
        )
        totals[2] = totals[2] + grad_first
        totals[3] = totals[3] + grad_second
        grad_conv = (grad_mixer * middle_part).reshape(seq_count, local_len, features)
        rim_back = from_behind(grad_conv[:, :2, :], "seq", -1)
        beyond = jnp.concatenate([grad_conv, rim_back], axis=1)
        grad_gated = (
            kernel[2] * beyond[:, :local_len]
            + kernel[1] * beyond[:, 1 : local_len + 1]
            + kernel[0] * beyond[:, 2:]
        ).reshape(row_count, features)
        grad_mixed = jnp.concatenate(
            [grad_gated * last_part, grad_mixer * conv_out, grad_gated * first_part], axis=1
        ).astype(jnp.bfloat16)
        grad_normed, grad_first, grad_second = adapted_back(
            grad_mixed, normed, low_in, weight_in, adapters[0], adapters[1], select
        )
        totals[0] = totals[0] + grad_first
        totals[1] = totals[1] + grad_second
        grad_input = grad_after + rms_back(grad_normed, gain_first, inverse_first, unit_first)
        input_grads.append(grad_input.astype(jnp.bfloat16).reshape(seq_count, local_len, features))
    summed = lax.psum(
        (
            totals[0],
            totals[1],
            totals[2],
            totals[3],
            totals[4],
            totals[5],
            totals[6],
            totals[7],
            totals[8],
            totals[9],
        ),
        ("fsdp", "seq"),
    )
    return (
        jnp.stack(outputs),
        jnp.stack(input_grads),
        summed[0],
        summed[1],
        summed[2],
        summed[3],
        summed[4],
        summed[5],
        summed[6],
        summed[7],
        summed[8],
        summed[9],
    )


def solution(mesh):
    return jax.shard_map(
        per_device,
        mesh=mesh,
        in_specs=(
            P(None, "fsdp", "seq", None),
            P(None, "fsdp", "seq", None),
            P(None, "fsdp"),
            P("fsdp", None),
            P("fsdp", None),
            P("fsdp", None),
            P("fsdp", None),
            P("fsdp", None),
            P(),
            P(),
            P(),
            P(),
            P(),
            P(),
            P(),
            P(),
            P(),
            P(),
            P(),
            P(),
            P(),
        ),
        out_specs=(
            P(None, "fsdp", "seq", None),
            P(None, "fsdp", "seq", None),
            P(),
            P(),
            P(),
            P(),
            P(),
            P(),
            P(),
            P(),
            P(),
            P(),
        ),
        check_vma=False,
    )
```

profile of v0, /device:TPU:0, one launch (start us, length us, event | category | flops | bytes accessed | tf_op | source)
XLA Modules:
  0.0 815.4 jit_solution(7204211921925107187)
XLA Ops:
  14.0 2.0 fusion.43
  19.3 55.6 %all-gather.6.cloned.1.call-done = bf16[1024,3072]{1,0:T(8,128)(2,1)} async-done(((bf16[64,3072]{1,0:T(8,128)(2,1)}), bf16[1024,3072]{1,0:T(8,128)(2,1)}) %all-gather.6.cloned.1.call-update) | async-done | bytes 6291472 | tf_op jit(solution)/shard_map/all_gather | solution.py:104
  74.9 5.9 fusion.106
  82.4 3.4 collective-permute-start.1
  85.8 3.6 fusion.111
  93.7 3.7 multiply_convert_fusion.15
  102.3 14.8 %all-gather.8.cloned.1.call-done = bf16[1024,1024]{1,0:T(8,128)(2,1)} async-done(((bf16[64,1024]{1,0:T(8,128)(2,1)}), bf16[1024,1024]{1,0:T(8,128)(2,1)}) %all-gather.8.cloned.1.call-update) | async-done | bytes 2097168 | tf_op jit(solution)/shard_map/all_gather | solution.py:105
  117.1 4.2 multiply_reduce_fusion.3
  127.3 72.4 %all-gather.12.cloned.1.call-done = bf16[1024,4608]{1,0:T(8,128)(2,1)} async-done(((bf16[64,4608]{1,0:T(8,128)(2,1)}), bf16[1024,4608]{1,0:T(8,128)(2,1)}) %all-gather.12.cloned.1.call-update) | async-done | bytes 9437200 | tf_op jit(solution)/shard_map/all_gather | solution.py:107
  199.6 7.7 fusion.121
  207.3 4.9 multiply_add_fusion.2
  212.2 69.2 %all-gather.14.cloned.1.call-done = bf16[4608,1024]{1,0:T(8,128)(2,1)} async-done(((bf16[288,1024]{1,0:T(8,128)(2,1)}), bf16[4608,1024]{1,0:T(8,128)(2,1)}) %all-gather.14.cloned.1.call-update) | async-done | bytes 9437200 | tf_op jit(solution)/shard_map/all_gather | solution.py:108
  281.4 8.3 %fusion.82 = f32[512,4608]{1,0:T(8,128)S(1)} fusion(bf16[4608,1024]{1,0:T(8,128)(2,1)} %all-gather.14.cloned.1.call-done, bf16[2,1,512,1024]{3,2,1,0:T(8,128)(2,1)} %param.22), kind=kOutput, calls=%fused_computation.178 | convolution fusion | flops 4831838208 | bytes 19922944 | tf_op jit(solution)/shard_map/dot_general | solution.py:22
  289.7 5.0 convolution_add_fusion.1
  294.7 68.5 %all-gather.10.cloned.1.call-done = bf16[1024,4608]{1,0:T(8,128)(2,1)} async-done(((bf16[64,4608]{1,0:T(8,128)(2,1)}), bf16[1024,4608]{1,0:T(8,128)(2,1)}) %all-gather.10.cloned.1.call-update) | async-done | bytes 9437200 | tf_op jit(solution)/shard_map/all_gather | solution.py:106
  363.1 11.0 %fusion.120 = f32[512,4608]{1,0:T(8,128)} fusion(bf16[512,1024]{1,0:T(8,128)(2,1)S(1)} %get-tuple-element.55, bf16[1024,4608]{1,0:T(8,128)(2,1)} %all-gather.10.cloned.1.call-done), kind=kOutput, calls=%fused_computation.222 | convolution fusion | flops 4831838208 | bytes 19922944 | tf_op jit(solution)/shard_map/dot_general | solution.py:18
  374.2 16.5 %multiply_convert_fusion.3 = (bf16[512,4608]{1,0:T(8,128)(2,1)}, bf16[512,4608]{1,0:T(8,128)(2,1)}, bf16[512,4608]{1,0:T(8,128)(2,1)S(1)}) fusion(f32[512,4608]{1,0:T(8,128)} %convolution_add_fusion.1, f32[512,4608]{1,0:T(8,128)} %multiply_add_fusion.2, f32[512,4608]{1,0:T(8,128)} %fusion.120, bf16[512,128]{1,0:T(8,128)(2,1)} %fusion.67, ...), kind=kOutput, calls=%fused_computation.3 | convolution fusion | flops 644087808 | bytes 43778048 | tf_op jit(solution)/shard_map/dot_general | solution.py:18
  390.7 2.2 copy-done.28
  392.9 3.5 fusion.63
  396.4 3.9 fusion.140
  400.3 2.2 fusion.139
  404.0 2.2 fusion.137
  411.9 7.6 fusion.125
  419.5 4.9 multiply_add_fusion
  424.4 7.9 fusion.77
  432.3 5.0 convolution_add_fusion
  437.3 11.0 %fusion.124 = f32[512,4608]{1,0:T(8,128)} fusion(bf16[512,1024]{1,0:T(8,128)(2,1)S(1)} %get-tuple-element.56, bf16[1024,4608]{1,0:T(8,128)(2,1)} %all-gather.10.cloned.1.call-done), kind=kOutput, calls=%fused_computation.226 | convolution fusion | flops 4831838208 | bytes 19922944 | tf_op jit(solution)/shard_map/dot_general | solution.py:18
  448.4 16.3 %multiply_convert_fusion.1 = (bf16[512,4608]{1,0:T(8,128)(2,1)S(1)}, bf16[512,4608]{1,0:T(8,128)(2,1)}, bf16[512,4608]{1,0:T(8,128)(2,1)}) fusion(f32[512,4608]{1,0:T(8,128)} %convolution_add_fusion, f32[512,4608]{1,0:T(8,128)} %multiply_add_fusion, f32[512,4608]{1,0:T(8,128)} %fusion.124, bf16[512,128]{1,0:T(8,128)(2,1)} %fusion.71, ...), kind=kOutput, calls=%fused_computation.1 | convolution fusion | flops 644087808 | bytes 43778048 | tf_op jit(solution)/shard_map/dot_general | solution.py:18
  464.6 5.8 fusion.61
  472.3 7.9 fusion.131
  480.2 7.8 fusion.133
  489.1 7.9 fusion.127
  497.0 8.0 fusion.129
  512.1 2.9 convolution_add_fusion.2
  515.0 2.2 fusion.3
  518.6 2.3 fusion.2
  528.0 1.9 multiply_convert_fusion.7
  529.9 1.8 collective-permute-start.3
  540.0 3.1 collective-permute-done.2
  543.2 3.9 multiply_convert_fusion.11
  553.8 1.8 fusion.4
  557.8 9.9 %fusion.122 = f32[512,1024]{1,0:T(8,128)S(1)} fusion(bf16[512,4608]{1,0:T(8,128)(2,1)} %copy-done.28, bf16[4608,1024]{1,0:T(8,128)(2,1)} %all-gather.14.cloned.1.call-done), kind=kOutput, calls=%fused_computation.224 | convolution fusion | flops 4831838208 | bytes 16252928 | tf_op jit(solution)/shard_map/dot_general | solution.py:18
  568.2 9.6 %fusion.126 = f32[512,1024]{1,0:T(8,128)S(1)} fusion(bf16[512,4608]{1,0:T(8,128)(2,1)} %get-tuple-element.39, bf16[4608,1024]{1,0:T(8,128)(2,1)} %all-gather.14.cloned.1.call-done), kind=kOutput, calls=%fused_computation.228 | convolution fusion | flops 4831838208 | bytes 16252928 | tf_op jit(solution)/shard_map/dot_general | solution.py:18
  581.6 3.5 add_multiply_fusion
  585.2 6.9 fusion.38
  594.7 198.8 %all-reduce.3.cloned.1.call-done = (f32[1024,128]{1,0:T(8,128)}, f32[128,3072]{1,0:T(8,128)}, f32[1024,128]{1,0:T(8,128)}, f32[128,1024]{1,0:T(8,128)}, f32[1024...) async-done(((f32[1024,128]{1,0:T(8,128)}, f32[128,3072]{1,0:T(8,128)}, ...) | async-done | bytes 11796496 | tf_op jit(solution)/shard_map/psum | solution.py:204
  793.6 1.9 copy.43
  795.5 2.8 copy.44
  (414 shorter events, 85.4 us)
Async XLA Ops:
  7.2 367.0 %copy-start = (bf16[128,4608]{1,0:T(8,128)(2,1)S(1)}, bf16[128,4608]{1,0:T(8,128)(2,1)}, u32[]{:S(2)}) copy-start(bf16[128,4608]{1,0:T(8,128)(2,1)} %param.37) | copy-start | bytes 3538948
  7.2 67.7 %all-gather.6.cloned.1.call-start = ((), (), s32[]{:S(2)}) async-start(), calls=%async_computation | async-start | bytes 6684672 | tf_op jit(solution)/shard_map/all_gather | solution.py:104
  7.9 8.1 copy-start.18
  8.0 8.1 copy-start.70
  8.0 109.1 %all-gather.8.cloned.1.call-start = ((), (), s32[]{:S(2)}) async-start(), calls=%async_computation.1 | async-start | bytes 2228224 | tf_op jit(solution)/shard_map/all_gather | solution.py:105
  8.7 190.9 %all-gather.12.cloned.1.call-start = ((), (), s32[]{:S(2)}) async-start(), calls=%async_computation.3 | async-start | bytes 10027008 | tf_op jit(solution)/shard_map/all_gather | solution.py:107
  9.5 271.9 %all-gather.14.cloned.1.call-start = ((), (), s32[]{:S(2)}) async-start(), calls=%async_computation.4 | async-start | bytes 10027008 | tf_op jit(solution)/shard_map/all_gather | solution.py:108
  10.0 353.1 %all-gather.10.cloned.1.call-start = ((), (), s32[]{:S(2)}) async-start(), calls=%async_computation.2 | async-start | bytes 10027008 | tf_op jit(solution)/shard_map/all_gather | solution.py:106
  10.6 783.0 %all-reduce.3.cloned.1.call-start = ((), (), s32[]{:S(2)}) async-start(), calls=%async_computation.5 | async-start | bytes 23592960 | tf_op jit(solution)/shard_map/psum | solution.py:204
  10.7 75.1 %copy-start.115 = (f32[1024]{0:T(1024)}, f32[1024]{0:T(1024)S(1)}, u32[]{:S(2)}) copy-start(f32[1024]{0:T(1024)S(1)} %convert_element_type.169) | copy-start | bytes 12292
  16.0 58.9 %copy-start.111 = (f32[512]{0:T(512)}, f32[512]{0:T(512)S(1)}, u32[]{:S(2)}) copy-start(f32[512]{0:T(512)S(1)} %add_rsqrt_fusion.1) | copy-start | bytes 6148
  16.1 69.7 %copy-start.113 = (f32[512]{0:T(512)}, f32[512]{0:T(512)S(1)}, u32[]{:S(2)}) copy-start(f32[512]{0:T(512)S(1)} %add_rsqrt_fusion.3) | copy-start | bytes 6148
  18.8 62.0 %copy-start.91 = (bf16[512,128]{1,0:T(8,128)(2,1)}, bf16[512,128]{1,0:T(8,128)(2,1)S(1)}, u32[]{:S(2)}) copy-start(bf16[512,128]{1,0:T(8,128)(2,1)S(1)} %fusion.69) | copy-start | bytes 393220
  18.8 56.1 %copy-start.24 = (bf16[2,1,512,1024]{3,2,1,0:T(8,128)(2,1)S(1)}, bf16[2,1,512,1024]{3,2,1,0:T(8,128)(2,1)}, u32[]{:S(2)}) copy-start(bf16[2,1,512,1024]{3,2,1,0:T(8,128)(2,1)} %param.21) | copy-start | bytes 6291460
  19.3 70.1 %copy-start.93 = (bf16[512,128]{1,0:T(8,128)(2,1)}, bf16[512,128]{1,0:T(8,128)(2,1)S(1)}, u32[]{:S(2)}) copy-start(bf16[512,128]{1,0:T(8,128)(2,1)S(1)} %fusion.65) | copy-start | bytes 393220
  74.9 10.9 %slice-start.18 = ((s8[6291456]{0:T(1024)(128)(4,1)}), s8[4194304]{0:T(1024)(128)(4,1)S(1)}, s32[]{:S(2)}) async-start(s8[6291456]{0:T(1024)(128)(4,1)} %bitcast.241), calls=%async_computation.24 | async-start | bytes 8388608
  81.8 11.9 %copy-start.2 = (f32[512,3072]{1,0:T(8,128)}, f32[512,3072]{1,0:T(8,128)S(1)}, u32[]{:S(2)}) copy-start(f32[512,3072]{1,0:T(8,128)S(1)} %multiply_add_fusion.4) | copy-start | bytes 18874372
  82.4 10.2 %collective-permute-start.1 = (f32[1,2,1024]{2,1,0:T(2,128)S(1)}, f32[1,2,1024]{2,1,0:T(2,128)S(1)}, u32[]{:S(2)}, u32[]{:S(2)}) collective-permute-start(f32[1,2,1024]{2,1,0:T(2,128)S(1)} %slice.129), channel_id=1, source_target_pairs={{0,1},{2,3},{4,5},{6,7},{8,9},{10,11},{12,13},{14,15},{16,17},{18,... | collective-permute-start | bytes 24584 | tf_op jit(solution)/shard_map/ppermute | solution.py:14
  91.0 2.7 collective-permute-start
  92.6 30.3 %copy-start.98 = (f32[1024]{0:T(1024)}, f32[1024]{0:T(1024)S(1)}, u32[]{:S(2)}) copy-start(f32[1024]{0:T(1024)S(1)} %convert_element_type.175) | copy-start | bytes 12292
  124.2 313.2 %copy-start.16 = (bf16[512,1024]{1,0:T(8,128)(2,1)}, bf16[512,1024]{1,0:T(8,128)(2,1)S(1)}, u32[]{:S(2)}) copy-start(bf16[512,1024]{1,0:T(8,128)(2,1)S(1)} %get-tuple-element.56) | copy-start | bytes 3145732
  126.2 293.3 %copy-start.49 = (bf16[512,128]{1,0:T(8,128)(2,1)}, bf16[512,128]{1,0:T(8,128)(2,1)S(1)}, u32[]{:S(2)}) copy-start(bf16[512,128]{1,0:T(8,128)(2,1)S(1)} %fusion.72) | copy-start | bytes 393220
  281.4 8.3 %copy-start.31 = (bf16[4608,128]{1,0:T(8,128)(2,1)S(1)}, bf16[4608,128]{1,0:T(8,128)(2,1)}, u32[]{:S(2)}) copy-start(bf16[4608,128]{1,0:T(8,128)(2,1)} %param.40) | copy-start | bytes 3538948
  281.4 8.3 %copy-start.76 = (bf16[512,128]{1,0:T(8,128)(2,1)S(1)}, bf16[512,128]{1,0:T(8,128)(2,1)}, u32[]{:S(2)}) copy-start(bf16[512,128]{1,0:T(8,128)(2,1)} %fusion.53) | copy-start | bytes 393220
  424.4 8.0 copy-start.32
  424.4 8.0 copy-start.74
  448.4 16.3 %copy-start.121 = (f32[128]{0:T(128)S(1)}, f32[128]{0:T(128)}, u32[]{:S(2)}) copy-start(f32[128]{0:T(128)} %copy-done.120) | copy-start | bytes 1540
  471.8 8.3 %slice-start.6 = ((s8[4718592]{0:T(1024)(128)(4,1)}), s8[4194304]{0:T(1024)(128)(4,1)S(1)}, s32[]{:S(2)}) async-start(s8[4718592]{0:T(1024)(128)(4,1)} %bitcast.223), calls=%async_computation.12 | async-start | bytes 8388608
  472.3 7.9 slice-start.7
  472.3 16.8 %slice-start.16 = ((s8[4718592]{0:T(1024)(128)(4,1)}), s8[4194304]{0:T(1024)(128)(4,1)S(1)}, s32[]{:S(2)}) async-start(s8[4718592]{0:T(1024)(128)(4,1)} %bitcast.233), calls=%async_computation.22 | async-start | bytes 8388608
  480.2 7.8 copy-start.5
  480.2 7.8 copy-start.67
  480.2 7.8 copy-start.99
  480.2 8.8 %slice-start.17 = ((s8[4718592]{0:T(1024)(128)(4,1)}), s8[524288]{0:T(1024)(128)(4,1)S(1)}, s32[]{:S(2)}) async-start(s8[4718592]{0:T(1024)(128)(4,1)} %bitcast.233), calls=%async_computation.23 | async-start | bytes 1048576
  488.1 8.9 %slice-start.12 = ((s8[4718592]{0:T(1024)(128)(4,1)}), s8[4194304]{0:T(1024)(128)(4,1)S(1)}, s32[]{:S(2)}) async-start(s8[4718592]{0:T(1024)(128)(4,1)} %bitcast.229), calls=%async_computation.18 | async-start | bytes 8388608
  489.1 7.9 slice-start.13
  497.0 8.0 copy-start.7
  497.0 8.0 copy-start.27
  497.0 8.0 copy-start.79
  497.0 8.0 copy-start.109
  507.8 16.9 %copy-start.11 = (f32[512,1024]{1,0:T(8,128)}, f32[512,1024]{1,0:T(8,128)S(1)}, u32[]{:S(2)}) copy-start(f32[512,1024]{1,0:T(8,128)S(1)} %get-tuple-element.45) | copy-start | bytes 6291460
  507.8 25.2 %copy-start.9 = (f32[512,1024]{1,0:T(8,128)}, f32[512,1024]{1,0:T(8,128)S(1)}, u32[]{:S(2)}) copy-start(f32[512,1024]{1,0:T(8,128)S(1)} %get-tuple-element.44) | copy-start | bytes 6291460
  529.9 10.2 %collective-permute-start.3 = (f32[1,2,1024]{2,1,0:T(2,128)S(1)}, f32[1,2,1024]{2,1,0:T(2,128)S(1)}, u32[]{:S(2)}, u32[]{:S(2)}) collective-permute-start(f32[1,2,1024]{2,1,0:T(2,128)S(1)} %slice.135), channel_id=1, source_target_pairs={{1,0},{3,2},{5,4},{7,6},{9,8},{11,10},{13,12},{15,14},{17,16},{19,... | collective-permute-start | bytes 24584 | tf_op jit(solution)/shard_map/ppermute | solution.py:14
  537.6 5.5 collective-permute-start.2
  557.7 10.0 %copy-start.8 = (f32[512,1024]{1,0:T(8,128)S(1)}, f32[512,1024]{1,0:T(8,128)}, u32[]{:S(2)}) copy-start(f32[512,1024]{1,0:T(8,128)} %copy-done.6) | copy-start | bytes 6291460
  557.8 10.0 %copy-start.71 = (bf16[128,1024]{1,0:T(8,128)(2,1)S(1)}, bf16[128,1024]{1,0:T(8,128)(2,1)}, u32[]{:S(2)}) copy-start(bf16[128,1024]{1,0:T(8,128)(2,1)} %param.41) | copy-start | bytes 786436
  567.7 12.9 %slice-start.20 = ((s8[6291456]{0:T(1024)(128)(4,1)}), s8[4194304]{0:T(1024)(128)(4,1)S(1)}, s32[]{:S(2)}) async-start(s8[6291456]{0:T(1024)(128)(4,1)} %bitcast.243), calls=%async_computation.26 | async-start | bytes 8388608
  568.2 12.5 %slice-start.21 = ((s8[6291456]{0:T(1024)(128)(4,1)}), s8[2097152]{0:T(1024)(128)(4,1)S(1)}, s32[]{:S(2)}) async-start(s8[6291456]{0:T(1024)(128)(4,1)} %bitcast.243), calls=%async_computation.27 | async-start | bytes 4194304
  (113 other events, 344.2 us)
Sparse Core Ops, SparseCore 0:
  10.3 64.5 all-gather.5
  77.1 39.9 all-gather.7
  119.4 80.2 all-gather.11
  201.8 79.5 all-gather.13
  283.5 79.5 all-gather.9
  557.9 235.6 all-reduce.2
where the time goes:
time: 823 us; the launch traced here: 815 us
  waiting for transfers between devices  487 us (59%)
  matrix products  252 us (31%)
  local copies, waits for them, and re-layouts  28.7 us (3%)
  other arithmetic  23.6 us (3%)
  between operations  16.2 us (2%)
    psum x1, waiting for transfers between devices, per_device(): lax.psum((totals[0], totals[1], totals[2], totals[3], totals[4], totals[5...  199 us
    dot_general x30, matrix products, forward_dot(): return jnp.dot(left_side, right_side, preferred_element_type=jnp.float32)  131 us
    dot_general x30, matrix products, against_dot(): lax.dot_general(left_side, right_side, (((1,), (1,)), ((), ())), preferre...  91.5 us
    all_gather x1, waiting for transfers between devices, per_device(): lax.all_gather(up_weight, 'fsdp', axis=0, tiled=True)  72.4 us
    all_gather x1, waiting for transfers between devices, per_device(): lax.all_gather(down_weight, 'fsdp', axis=0, tiled=True)  69.2 us
    all_gather x1, waiting for transfers between devices, per_device(): lax.all_gather(gate_weight, 'fsdp', axis=0, tiled=True)  68.5 us
    all_gather x1, waiting for transfers between devices, per_device(): lax.all_gather(in_weight, 'fsdp', axis=0, tiled=True)  55.6 us
    dot_general x20, matrix products, outer_dot(): lax.dot_general(left_side, right_side, (((0,), (0,)), ((), ())), preferre...  30 us
  transfers between devices with their start and end apart: 10, of which 8 were waited for; matrix products, arithmetic and copies ran while one was open for 13% of the time, Pallas kernels for 0%

commit v1 on v0

--- a/solution.py
+++ b/solution.py
@@ -202,19 +202,22 @@
         grad_input = grad_after + rms_back(grad_normed, gain_first, inverse_first, unit_first)
         input_grads.append(grad_input.astype(jnp.bfloat16).reshape(seq_count, local_len, features))
     summed = lax.psum(
-        (
-            totals[0],
-            totals[1],
-            totals[2],
-            totals[3],
-            totals[4],
-            totals[5],
-            totals[6],
-            totals[7],
-            totals[8],
-            totals[9],
+        lax.psum(
+            (
+                totals[0],
+                totals[1],
+                totals[2],
+                totals[3],
+                totals[4],
+                totals[5],
+                totals[6],
+                totals[7],
+                totals[8],
+                totals[9],
+            ),
+            "seq",
         ),
-        ("fsdp", "seq"),
+        "fsdp",
     )
     return (
         jnp.stack(outputs),

time: 823 us -> 1090 us (1.32)
  waiting for transfers between devices: 487 us -> 753 us
    psum x0 -> x1, waiting for transfers between devices: none -> 192 us  [per_device(): lax.psum(lax.psum((totals[0], totals[1], totals[2], totals[3], totals[4],...]
    psum x1, waiting for transfers between devices: 199 us -> 273 us  [per_device(): lax.psum((totals[0], totals[1], totals[2], totals[3], totals[4], totals[5...]
  transfers between devices with their start and end apart: 10 -> 11, of which waited for: 8 -> 9; matrix products, arithmetic and copies ran while one was open for 13% -> 10% of each run, Pallas kernels for 0% -> 0%
where the time goes in v1:
time: 1090 us; the launch traced here: 1080 us
  waiting for transfers between devices  753 us (69%)
  matrix products  252 us (23%)
  local copies, waits for them, and re-layouts  28.8 us (3%)
  other arithmetic  23.5 us (2%)
  between operations  16.3 us (1%)
    psum x1, waiting for transfers between devices, per_device(): lax.psum((totals[0], totals[1], totals[2], totals[3], totals[4], totals[5...  273 us
    psum x1, waiting for transfers between devices, per_device(): lax.psum(lax.psum((totals[0], totals[1], totals[2], totals[3], totals[4],...  192 us
    dot_general x30, matrix products, forward_dot(): return jnp.dot(left_side, right_side, preferred_element_type=jnp.float32)  131 us
    dot_general x30, matrix products, against_dot(): lax.dot_general(left_side, right_side, (((1,), (1,)), ((), ())), preferre...  91.4 us
    all_gather x1, waiting for transfers between devices, per_device(): lax.all_gather(up_weight, 'fsdp', axis=0, tiled=True)  72.4 us
    all_gather x1, waiting for transfers between devices, per_device(): lax.all_gather(down_weight, 'fsdp', axis=0, tiled=True)  69.1 us
    all_gather x1, waiting for transfers between devices, per_device(): lax.all_gather(gate_weight, 'fsdp', axis=0, tiled=True)  68.5 us
    all_gather x1, waiting for transfers between devices, per_device(): lax.all_gather(in_weight, 'fsdp', axis=0, tiled=True)  55.6 us
  transfers between devices with their start and end apart: 11, of which 9 were waited for; matrix products, arithmetic and copies ran while one was open for 10% of the time, Pallas kernels for 0%

profile of v1, /device:TPU:0, one launch (start us, length us, event | category | flops | bytes accessed | tf_op | source)
XLA Modules:
  0.0 1082.4 jit_solution(7550105549889263009)
XLA Ops:
  14.0 2.0 fusion.43
  19.3 55.6 %all-gather.6.cloned.1.call-done = bf16[1024,3072]{1,0:T(8,128)(2,1)} async-done(((bf16[64,3072]{1,0:T(8,128)(2,1)}), bf16[1024,3072]{1,0:T(8,128)(2,1)}) %all-gather.6.cloned.1.call-update) | async-done | bytes 6291472 | tf_op jit(solution)/shard_map/all_gather | solution.py:104
  74.9 5.9 fusion.106
  82.4 3.4 collective-permute-start.1
  85.8 3.6 fusion.111
  93.7 3.7 multiply_convert_fusion.15
  102.3 14.8 %all-gather.8.cloned.1.call-done = bf16[1024,1024]{1,0:T(8,128)(2,1)} async-done(((bf16[64,1024]{1,0:T(8,128)(2,1)}), bf16[1024,1024]{1,0:T(8,128)(2,1)}) %all-gather.8.cloned.1.call-update) | async-done | bytes 2097168 | tf_op jit(solution)/shard_map/all_gather | solution.py:105
  117.1 4.2 multiply_reduce_fusion.3
  127.3 72.4 %all-gather.12.cloned.1.call-done = bf16[1024,4608]{1,0:T(8,128)(2,1)} async-done(((bf16[64,4608]{1,0:T(8,128)(2,1)}), bf16[1024,4608]{1,0:T(8,128)(2,1)}) %all-gather.12.cloned.1.call-update) | async-done | bytes 9437200 | tf_op jit(solution)/shard_map/all_gather | solution.py:107
  199.6 7.7 fusion.121
  207.3 4.9 multiply_add_fusion.2
  212.2 69.1 %all-gather.14.cloned.1.call-done = bf16[4608,1024]{1,0:T(8,128)(2,1)} async-done(((bf16[288,1024]{1,0:T(8,128)(2,1)}), bf16[4608,1024]{1,0:T(8,128)(2,1)}) %all-gather.14.cloned.1.call-update) | async-done | bytes 9437200 | tf_op jit(solution)/shard_map/all_gather | solution.py:108
  281.4 8.3 fusion.82
  289.7 5.0 convolution_add_fusion.1
  294.6 68.5 %all-gather.10.cloned.1.call-done = bf16[1024,4608]{1,0:T(8,128)(2,1)} async-done(((bf16[64,4608]{1,0:T(8,128)(2,1)}), bf16[1024,4608]{1,0:T(8,128)(2,1)}) %all-gather.10.cloned.1.call-update) | async-done | bytes 9437200 | tf_op jit(solution)/shard_map/all_gather | solution.py:106
  363.1 11.0 %fusion.120 = f32[512,4608]{1,0:T(8,128)} fusion(bf16[512,1024]{1,0:T(8,128)(2,1)S(1)} %get-tuple-element.65, bf16[1024,4608]{1,0:T(8,128)(2,1)} %all-gather.10.cloned.1.call-done), kind=kOutput, calls=%fused_computation.222 | convolution fusion | flops 4831838208 | bytes 19922944 | tf_op jit(solution)/shard_map/dot_general | solution.py:18
  374.2 16.4 %multiply_convert_fusion.3 = (bf16[512,4608]{1,0:T(8,128)(2,1)}, bf16[512,4608]{1,0:T(8,128)(2,1)}, bf16[512,4608]{1,0:T(8,128)(2,1)S(1)}) fusion(f32[512,4608]{1,0:T(8,128)} %convolution_add_fusion.1, f32[512,4608]{1,0:T(8,128)} %multiply_add_fusion.2, f32[512,4608]{1,0:T(8,128)} %fusion.120, bf16[512,128]{1,0:T(8,128)(2,1)} %fusion.67, ...), kind=kOutput, calls=%fused_computation.3 | convolution fusion | flops 644087808 | bytes 43778048 | tf_op jit(solution)/shard_map/dot_general | solution.py:18
  390.6 2.2 copy-done.28
  392.8 3.5 fusion.63
  396.3 3.9 fusion.140
  400.3 2.2 fusion.139
  403.9 2.2 fusion.137
  411.8 7.6 fusion.125
  419.4 4.9 multiply_add_fusion
  424.3 7.9 fusion.77
  432.3 5.0 convolution_add_fusion
  437.3 11.0 %fusion.124 = f32[512,4608]{1,0:T(8,128)} fusion(bf16[512,1024]{1,0:T(8,128)(2,1)S(1)} %get-tuple-element.66, bf16[1024,4608]{1,0:T(8,128)(2,1)} %all-gather.10.cloned.1.call-done), kind=kOutput, calls=%fused_computation.226 | convolution fusion | flops 4831838208 | bytes 19922944 | tf_op jit(solution)/shard_map/dot_general | solution.py:18
  448.3 16.2 %multiply_convert_fusion.1 = (bf16[512,4608]{1,0:T(8,128)(2,1)S(1)}, bf16[512,4608]{1,0:T(8,128)(2,1)}, bf16[512,4608]{1,0:T(8,128)(2,1)}) fusion(f32[512,4608]{1,0:T(8,128)} %convolution_add_fusion, f32[512,4608]{1,0:T(8,128)} %multiply_add_fusion, f32[512,4608]{1,0:T(8,128)} %fusion.124, bf16[512,128]{1,0:T(8,128)(2,1)} %fusion.71, ...), kind=kOutput, calls=%fused_computation.1 | convolution fusion | flops 644087808 | bytes 43778048 | tf_op jit(solution)/shard_map/dot_general | solution.py:18
  464.5 5.8 fusion.61
  472.2 7.9 fusion.131
  480.2 7.8 fusion.133
  489.0 7.9 fusion.127
  497.0 8.0 fusion.129
  512.0 2.9 convolution_add_fusion.2
  514.9 2.2 fusion.3
  518.5 2.3 fusion.2
  527.9 1.9 multiply_convert_fusion.7
  529.7 1.8 collective-permute-start.3
  539.9 3.1 collective-permute-done.2
  543.0 3.8 multiply_convert_fusion.11
  557.8 273.4 %all-reduce.7.cloned.1.call-done = (f32[1024,128]{1,0:T(8,128)}, f32[128,3072]{1,0:T(8,128)}, f32[1024,128]{1,0:T(8,128)}, f32[128,1024]{1,0:T(8,128)}, f32[1024...) async-done(((f32[1024,128]{1,0:T(8,128)}, f32[128,3072]{1,0:T(8,128)}, ...) | async-done | bytes 11796496 | tf_op jit(solution)/shard_map/psum | solution.py:205
  831.3 9.1 fusion.122
  840.9 10.7 fusion.126
  855.5 3.5 add_multiply_fusion
  859.1 6.8 fusion.38
  868.6 192.0 %all-reduce.5.cloned.1.call-done = (f32[1024,128]{1,0:T(8,128)}, f32[128,3072]{1,0:T(8,128)}, f32[1024,128]{1,0:T(8,128)}, f32[128,1024]{1,0:T(8,128)}, f32[1024...) async-done(((f32[1024,128]{1,0:T(8,128)}, f32[128,3072]{1,0:T(8,128)}, ...) | async-done | bytes 11796496 | tf_op jit(solution)/shard_map/psum | solution.py:204
  1060.6 1.9 copy.53
  1062.5 2.8 copy.54
  (417 shorter events, 87.5 us)
Async XLA Ops:
  7.2 367.0 %copy-start = (bf16[128,4608]{1,0:T(8,128)(2,1)S(1)}, bf16[128,4608]{1,0:T(8,128)(2,1)}, u32[]{:S(2)}) copy-start(bf16[128,4608]{1,0:T(8,128)(2,1)} %param.37) | copy-start | bytes 3538948
  7.2 67.7 %all-gather.6.cloned.1.call-start = ((), (), s32[]{:S(2)}) async-start(), calls=%async_computation | async-start | bytes 6684672 | tf_op jit(solution)/shard_map/all_gather | solution.py:104
  7.9 8.1 copy-start.18
  8.0 8.1 copy-start.70
  8.0 109.1 %all-gather.8.cloned.1.call-start = ((), (), s32[]{:S(2)}) async-start(), calls=%async_computation.1 | async-start | bytes 2228224 | tf_op jit(solution)/shard_map/all_gather | solution.py:105
  8.7 190.9 %all-gather.12.cloned.1.call-start = ((), (), s32[]{:S(2)}) async-start(), calls=%async_computation.3 | async-start | bytes 10027008 | tf_op jit(solution)/shard_map/all_gather | solution.py:107
  9.5 271.9 %all-gather.14.cloned.1.call-start = ((), (), s32[]{:S(2)}) async-start(), calls=%async_computation.4 | async-start | bytes 10027008 | tf_op jit(solution)/shard_map/all_gather | solution.py:108
  10.0 353.1 %all-gather.10.cloned.1.call-start = ((), (), s32[]{:S(2)}) async-start(), calls=%async_computation.2 | async-start | bytes 10027008 | tf_op jit(solution)/shard_map/all_gather | solution.py:106
  10.6 820.6 %all-reduce.7.cloned.1.call-start = ((), (), s32[]{:S(2)}) async-start(), calls=%async_computation.6 | async-start | bytes 23592960 | tf_op jit(solution)/shard_map/psum | solution.py:205
  10.7 75.1 %copy-start.115 = (f32[1024]{0:T(1024)}, f32[1024]{0:T(1024)S(1)}, u32[]{:S(2)}) copy-start(f32[1024]{0:T(1024)S(1)} %convert_element_type.169) | copy-start | bytes 12292
  16.0 58.9 %copy-start.111 = (f32[512]{0:T(512)}, f32[512]{0:T(512)S(1)}, u32[]{:S(2)}) copy-start(f32[512]{0:T(512)S(1)} %add_rsqrt_fusion.1) | copy-start | bytes 6148
  16.1 69.7 %copy-start.113 = (f32[512]{0:T(512)}, f32[512]{0:T(512)S(1)}, u32[]{:S(2)}) copy-start(f32[512]{0:T(512)S(1)} %add_rsqrt_fusion.3) | copy-start | bytes 6148
  18.8 62.0 %copy-start.91 = (bf16[512,128]{1,0:T(8,128)(2,1)}, bf16[512,128]{1,0:T(8,128)(2,1)S(1)}, u32[]{:S(2)}) copy-start(bf16[512,128]{1,0:T(8,128)(2,1)S(1)} %fusion.69) | copy-start | bytes 393220
  18.8 56.1 %copy-start.24 = (bf16[2,1,512,1024]{3,2,1,0:T(8,128)(2,1)S(1)}, bf16[2,1,512,1024]{3,2,1,0:T(8,128)(2,1)}, u32[]{:S(2)}) copy-start(bf16[2,1,512,1024]{3,2,1,0:T(8,128)(2,1)} %param.21) | copy-start | bytes 6291460
  19.3 70.1 %copy-start.93 = (bf16[512,128]{1,0:T(8,128)(2,1)}, bf16[512,128]{1,0:T(8,128)(2,1)S(1)}, u32[]{:S(2)}) copy-start(bf16[512,128]{1,0:T(8,128)(2,1)S(1)} %fusion.65) | copy-start | bytes 393220
  74.9 10.9 %slice-start.18 = ((s8[6291456]{0:T(1024)(128)(4,1)}), s8[4194304]{0:T(1024)(128)(4,1)S(1)}, s32[]{:S(2)}) async-start(s8[6291456]{0:T(1024)(128)(4,1)} %bitcast.241), calls=%async_computation.25 | async-start | bytes 8388608
  81.8 11.9 %copy-start.2 = (f32[512,3072]{1,0:T(8,128)}, f32[512,3072]{1,0:T(8,128)S(1)}, u32[]{:S(2)}) copy-start(f32[512,3072]{1,0:T(8,128)S(1)} %multiply_add_fusion.4) | copy-start | bytes 18874372
  82.4 10.2 collective-permute-start.1
  91.0 2.7 collective-permute-start
  92.6 30.3 %copy-start.98 = (f32[1024]{0:T(1024)}, f32[1024]{0:T(1024)S(1)}, u32[]{:S(2)}) copy-start(f32[1024]{0:T(1024)S(1)} %convert_element_type.175) | copy-start | bytes 12292
  124.2 313.1 %copy-start.16 = (bf16[512,1024]{1,0:T(8,128)(2,1)}, bf16[512,1024]{1,0:T(8,128)(2,1)S(1)}, u32[]{:S(2)}) copy-start(bf16[512,1024]{1,0:T(8,128)(2,1)S(1)} %get-tuple-element.66) | copy-start | bytes 3145732
  126.2 293.2 %copy-start.49 = (bf16[512,128]{1,0:T(8,128)(2,1)}, bf16[512,128]{1,0:T(8,128)(2,1)S(1)}, u32[]{:S(2)}) copy-start(bf16[512,128]{1,0:T(8,128)(2,1)S(1)} %fusion.72) | copy-start | bytes 393220
  281.4 8.3 copy-start.31
  281.4 8.3 copy-start.76
  424.3 8.0 copy-start.32
  424.3 8.0 copy-start.74
  448.3 16.2 %copy-start.121 = (f32[128]{0:T(128)S(1)}, f32[128]{0:T(128)}, u32[]{:S(2)}) copy-start(f32[128]{0:T(128)} %copy-done.120) | copy-start | bytes 1540
  471.7 8.3 slice-start.6
  472.2 7.9 slice-start.7
  472.2 16.8 %slice-start.16 = ((s8[4718592]{0:T(1024)(128)(4,1)}), s8[4194304]{0:T(1024)(128)(4,1)S(1)}, s32[]{:S(2)}) async-start(s8[4718592]{0:T(1024)(128)(4,1)} %bitcast.233), calls=%async_computation.23 | async-start | bytes 8388608
  480.1 7.8 copy-start.5
  480.1 7.8 copy-start.67
  480.1 8.8 slice-start.17
  488.0 8.9 slice-start.12
  489.0 7.9 slice-start.13
  496.9 8.0 copy-start.7
  496.9 8.0 copy-start.27
  496.9 8.0 copy-start.79
  496.9 8.0 copy-start.109
  507.7 16.9 %copy-start.11 = (f32[512,1024]{1,0:T(8,128)}, f32[512,1024]{1,0:T(8,128)S(1)}, u32[]{:S(2)}) copy-start(f32[512,1024]{1,0:T(8,128)S(1)} %get-tuple-element.55) | copy-start | bytes 6291460
  507.7 25.1 %copy-start.9 = (f32[512,1024]{1,0:T(8,128)}, f32[512,1024]{1,0:T(8,128)S(1)}, u32[]{:S(2)}) copy-start(f32[512,1024]{1,0:T(8,128)S(1)} %get-tuple-element.54) | copy-start | bytes 6291460
  529.7 10.2 collective-permute-start.3
  537.5 5.5 collective-permute-start.2
  557.6 503.0 %all-reduce.5.cloned.1.call-start = ((), (), s32[]{:S(2)}) async-start(), calls=%async_computation.5 | async-start | bytes 23592960 | tf_op jit(solution)/shard_map/psum | solution.py:204
  831.3 9.2 copy-start.8
  831.3 9.2 copy-start.71
  840.4 14.0 %slice-start.20 = ((s8[6291456]{0:T(1024)(128)(4,1)}), s8[4194304]{0:T(1024)(128)(4,1)S(1)}, s32[]{:S(2)}) async-start(s8[6291456]{0:T(1024)(128)(4,1)} %bitcast.243), calls=%async_computation.27 | async-start | bytes 8388608
  840.9 13.6 %slice-start.21 = ((s8[6291456]{0:T(1024)(128)(4,1)}), s8[2097152]{0:T(1024)(128)(4,1)S(1)}, s32[]{:S(2)}) async-start(s8[6291456]{0:T(1024)(128)(4,1)} %bitcast.243), calls=%async_computation.28 | async-start | bytes 4194304
  (114 other events, 352.1 us)
Sparse Core Ops, SparseCore 0:
  10.3 64.5 all-gather.5
  77.1 39.9 all-gather.7
  119.4 80.2 all-gather.11
  201.8 79.5 all-gather.13
  283.5 79.5 all-gather.9
  557.7 273.4 all-reduce.6
  836.2 224.3 all-reduce.4
